TPU v7x, 128 devices: a whole 4x4x4 slice. The times are simulated.
128 devices in a mesh: gx: 8 (over y, core), gy: 16 (over z, x).
Axes of the slice: x: 4, y: 4, z: 4, core: 2. Of those that a mesh axis runs over, the one named last changes fastest.
Arguments:
- charges: bfloat16 [2048, 256, 64], P(('gx', 'gy')), may hold values from -6 to 6
- leaf_basis: bfloat16 [2048, 256, 64], P(('gx', 'gy')), may hold values from -0.375 to 0.375
- transfer: bfloat16 [128, 24, 64, 64], P(('gx', 'gy')), may hold values from -0.5 to 0.5
- near_blocks: bfloat16 [2048, 6, 256, 256], P(('gx', 'gy')), may hold values from -0.15625 to 0.15625
- near_source: int32 [2048, 6], P(('gx', 'gy')), may hold values from 0 to 2047, as said below
- coupling: bfloat16 [128, 128, 6, 64, 64], P(('gx', 'gy')), may hold values from -0.25 to 0.25
- send_cluster: int32 [128, 128, 6], P(('gx', 'gy')), may hold values from 0 to 27, as said below
- target_cluster: int32 [128, 128, 6], P(('gx', 'gy')), may hold values from 0 to 28, as said below
Outputs:
- potential: bfloat16 [2048, 256, 64], P(('gx', 'gy'))
Inputs may be any that keep to these rules, and one draw needn't show every extreme that they name: `near_source`: leaf l's first source is l itself; the others are distinct offsets o with 0 < |o| <= 8, giving leaf l + o clipped to the range of leaves. send_cluster[p, d, c] is a cluster of device p in the numbering of the steps, on the same level as target_cluster[d, p, c] when that slot is used. target_cluster[d, p, c] is the cluster of device d that receives the slot; the value 28 marks an empty slot. Between devices whose indices differ by at most one all 6 slots are used.
All inputs are finite; a program needn't handle non-finite values.
Results may differ from a plain program's by a relative error of at most 0.0055.
Values may be sent and summed in bfloat16 or wider, within the bound.
No kernel may reach another device: no remote copies, remote signals or barrier semaphores. Data moves between devices by JAX's collectives and lax.ppermute only.
A program may use at most 192 MiB of HBM per device.

v0:
```python
import jax
import jax.numpy as jnp
from jax import lax
from jax.sharding import PartitionSpec as P

LEVELS = 3


def cut_along(shard, dim, length):
    before, after = (shard.shape[:dim], shard.shape[dim + 1 :])
    return jnp.moveaxis(shard.reshape(*before, length, -1, *after), dim, 0)


def laid_out(tiles, dim):
    dims = list(tiles.shape[1:])
    dims[dim] *= tiles.shape[0]
    return jnp.moveaxis(tiles, 0, dim).reshape(dims)


def exchange_both(shard, axis, axes, splits, concats):
    sizes = [lax.axis_size(a) for a in axes]
    tiles = cut_along(shard, splits[0], sizes[0])
    tiles = jnp.moveaxis(cut_along(tiles, splits[1] + 1, sizes[1]), 0, 1)
    inside = tiles.shape[2:]
    tiles = tiles.reshape(-1, *inside)
    tiles = lax.all_to_all(tiles, axis, split_axis=0, concat_axis=0, tiled=True)
    tiles = laid_out(tiles.reshape(*sizes, *inside), concats[0] + 1)
    return laid_out(tiles, concats[1])


def with_halo(shard, sides, width):
    edges = {}
    for axis, dim in sides:
        size, length = (lax.axis_size(axis), shard.shape[dim])
        up = [(i, (i + 1) % size) for i in range(size - 1)]
        last = lax.slice_in_dim(shard, length - width, length, axis=dim)
        initial = lax.slice_in_dim(shard, 0, width, axis=dim)
        edges[dim] = (
            lax.ppermute(last, axis, up),
            lax.ppermute(initial, axis, [(b, a) for a, b in up]),
        )
    done = []
    for _, dim in sides:
        low, high = edges[dim]
        around = [(width, width) if d in done else (0, 0) for d in range(shard.ndim)]
        shard = jnp.concatenate([jnp.pad(low, around), shard, jnp.pad(high, around)], axis=dim)
        done.append(dim)
    return shard


def shards(
    charges, leaf_basis, transfer, near_blocks, near_source, coupling, send_cluster, target_cluster
):
    highest = lax.Precision.HIGHEST
    single = jnp.float32
    leaves = charges.shape[0]
    panels = charges.shape[1]
    rank = leaf_basis.shape[2]
    width = charges.shape[2]
    peers = send_cluster.shape[1]
    slots = send_cluster.shape[2]
    first_level = jnp.einsum("lpk,lpr->lkr", leaf_basis, charges, preferred_element_type=single)
    levels = [first_level.astype(jnp.bfloat16)]
    bounds = []
    offset = 0
    for depth in range(LEVELS - 1):
        members = leaves >> depth
        bounds.append((offset, members))
        lifted = jnp.einsum(
            "ckj,ckr->cjr",
            transfer[0, offset : offset + members],
            levels[-1],
            preferred_element_type=single,
        )
        levels.append(lifted.reshape(members // 2, 2, rank, width).sum(axis=1).astype(jnp.bfloat16))
        offset = offset + members
    bounds.append((offset, leaves >> LEVELS - 1))
    clusters = offset + (leaves >> LEVELS - 1)
    upward_flat = jnp.concatenate(levels, axis=0).reshape(clusters, rank * width)
    picker = (send_cluster[0].reshape(-1)[:, None] == jnp.arange(clusters)[None, :]).astype(
        jnp.bfloat16
    )
    packed = (
        jnp.dot(picker, upward_flat, preferred_element_type=single)
        .astype(jnp.bfloat16)
        .reshape(peers, slots, rank * width)
    )
    outer = lax.axis_size("gx")
    inner = lax.axis_size("gy")
    shaped = packed.reshape(outer, inner, slots, rank * width)
    fetched = exchange_both(shaped, ("gx", "gy"), ("gx", "gy"), (0, 1), (0, 1)).reshape(
        peers, slots, rank, width
    )
    products = jnp.einsum("pckj,pcjr->pckr", coupling[0], fetched, preferred_element_type=single)
    selector = (target_cluster[0].reshape(-1)[None, :] == jnp.arange(clusters)[:, None]).astype(
        single
    )
    far_field = jnp.dot(
        selector, products.reshape(peers * slots, rank * width), precision=highest
    ).reshape(clusters, rank, width)
    down = [far_field[lo : lo + size] for lo, size in bounds]
    for depth in range(LEVELS - 2, -1, -1):
        lo, size = bounds[depth]
        spread = jnp.repeat(down[depth + 1], 2, axis=0)
        matrices = transfer[0, lo : lo + size].astype(single)
        down[depth] = down[depth] + jnp.einsum("ckj,cjr->ckr", matrices, spread, precision=highest)
    far_leaf = jnp.einsum("lpk,lkr->lpr", leaf_basis.astype(single), down[0], precision=highest)
    reach = leaves // 2
    padded = with_halo(charges, ((("gx", "gy"), 0),), reach)
    window = leaves + 2 * reach
    padded_flat = padded.reshape(window, panels * width)
    first_leaf = lax.axis_index(("gx", "gy")) * leaves
    local_rows = near_source - first_leaf + reach
    chooser = (local_rows.reshape(-1)[:, None] == jnp.arange(window)[None, :]).astype(jnp.bfloat16)
    gathered = jnp.dot(chooser, padded_flat, preferred_element_type=single).astype(jnp.bfloat16)
    gathered = gathered.reshape(leaves, near_source.shape[1], panels, width)
    near_field = jnp.einsum("lspq,lsqr->lpr", near_blocks, gathered, preferred_element_type=single)
    return (near_field + far_leaf).astype(jnp.bfloat16)


def solution(mesh):
    placed = (
        P(("gx", "gy"), None, None),
        P(("gx", "gy"), None, None),
        P(("gx", "gy"), None, None, None),
        P(("gx", "gy"), None, None, None),
        P(("gx", "gy"), None),
        P(("gx", "gy"), None, None, None, None),
        P(("gx", "gy"), None, None),
        P(("gx", "gy"), None, None),
    )
    return jax.shard_map(
        shards, mesh=mesh, in_specs=placed, out_specs=P(("gx", "gy"), None, None), check_vma=False
    )
```

profile of v0, /device:TPU:106, one launch (start us, length us, event | category | flops | bytes accessed | tf_op | source)
XLA Modules:
  0.0 273.8 jit_solution(18345869909550667426)
XLA Ops:
  0.0 1.0 copy-done
  1.0 1.3 convolution_convert_fusion.2
  2.4 1.2 bitcast_reduce_fusion
  3.7 1.1 bitcast_reduce_fusion.1
  6.4 4.5 %convolution_convert_fusion.1 = bf16[768,4096]{1,0:T(8,128)(2,1)} fusion(bf16[28,4096]{1,0:T(8,128)(2,1)S(1)} %reshape.41, s32[768]{0:T(1024)S(1)} %eq.53), kind=kOutput, calls=%fused_computation.4 | convolution fusion | flops 179328000 | bytes 6523904 | tf_op jit(solution)/shard_map/dot_general | solution.py:84
  10.9 10.2 %reshape_transpose_transpose_reshape_reshape_reshape_reshape.3 = bf16[128,1,1,6,4096]{4,3,0,2,1:T(8,128)(2,1)} reshape(bf16[768,4096]{1,0:T(8,128)(2,1)} %convolution_convert_fusion.1) | data formatting | bytes 12582912 | tf_op jit(solution)/shard_map/reshape;transpose;transpose;reshape;reshape;reshape;reshape | solution.py:25
  21.1 10.2 %all-to-all-start = ((bf16[128,1,1,6,4096]{4,3,2,1,0:T(8,128)(2,1)}), bf16[128,1,1,6,4096]{4,3,2,1,0:T(8,128)(2,1)}, u32[]{:S(2)}, u32[]{:S(2)}) async-start(bf16[128,1,1,6,4096]{4,3,2,1,0:T(8,128)(2,1)} %bitcast.69), calls=%async_computation | async-start | bytes 16777216 | tf_op jit(solution)/shard_map/all_to_all | solution.py:26
  31.4 3.4 %collective-permute-start = (bf16[8,256,64]{1,2,0:T(8,128)(2,1)S(1)}, bf16[8,256,64]{1,2,0:T(8,128)(2,1)S(1)}, u32[]{:S(2)}, u32[]{:S(2)}) collective-permute-start(bf16[8,256,64]{1,2,0:T(8,128)(2,1)S(1)} %get-tuple-element.5), channel_id=1, source_target_pairs={{0,1},{1,2},{2,3},{3,4},{4,5},{5,6},{6,7},{7,8},{8,9},{9,10},{10,1... | collective-permute-start | bytes 786440 | tf_op jit(solution)/shard_map/ppermute | solution.py:39
  34.8 2.6 collective-permute-start.1
  37.5 18.5 %copy.45 = bf16[128,6,64,64]{3,2,1,0:T(8,128)(2,1)} copy(bf16[128,6,64,64]{0,3,2,1:T(8,128)(2,1)} %bitcast.71) | data formatting | bytes 12582912 | tf_op jit(solution)/shard_map/squeeze | solution.py:94
  56.4 85.8 %collective-permute-done = bf16[8,256,64]{1,2,0:T(8,128)(2,1)S(1)} collective-permute-done((bf16[8,256,64]{1,2,0:T(8,128)(2,1)S(1)}, bf16[8,256,64]{1,2,0:T(8,128)(2,1)S(1)}, u32[]{:S(2)}, u32[]{:S(2)}) %collective-permute-start) | collective-permute-done | bytes 262176 | tf_op jit(solution)/shard_map/ppermute | solution.py:39
  142.3 1.1 pad_maximum_fusion
  143.4 2.0 copy.34
  145.4 2.5 reshape.37
  147.9 3.9 %convolution_convert_fusion = bf16[96,16384]{1,0:T(8,128)(2,1)} fusion(bf16[32,16384]{1,0:T(8,128)(2,1)} %reshape.37, s32[96]{0:T(128)S(1)} %eq.45), kind=kOutput, calls=%fused_computation | convolution fusion | flops 102239232 | bytes 4194688 | tf_op jit(solution)/shard_map/dot_general | solution.py:115
  151.7 8.9 %reshape.38 = bf16[16,6,256,64]{3,2,1,0:T(8,128)(2,1)} reshape(bf16[96,16384]{1,0:T(8,128)(2,1)} %convolution_convert_fusion) | data formatting | bytes 6291456 | tf_op jit(solution)/shard_map/reshape | solution.py:116
  160.7 8.5 %convolution_bitcast_fusion = f32[16,64,256]{2,1,0:T(8,128)S(1)} fusion(bf16[16,6,256,64]{3,2,1,0:T(8,128)(2,1)} %reshape.38, bf16[16,6,256,256]{3,2,1,0:T(8,128)(2,1)} %param.11), kind=kOutput, calls=%fused_computation.7 | convolution fusion | flops 805306368 | bytes 16777216 | tf_op jit(solution)/shard_map/lspq,lsqr->lpr/dot_general | solution.py:117
  169.2 9.5 %copy.61 = bf16[8,16,1,1,6,4096]{5,1,0,4,3,2:T(8,128)(2,1)} copy(bf16[8,16,1,1,6,4096]{5,4,1,0,3,2:T(8,128)(2,1)} %bitcast.9) | data formatting | bytes 12582912 | tf_op jit(solution)/shard_map/reshape | solution.py:27
  178.7 17.9 %reshape_reshape.3 = bf16[128,6,64,64]{3,2,0,1:T(8,128)(2,1)} reshape(bf16[8,16,1,6,4096]{4,1,0,3,2:T(8,128)(2,1)} %bitcast.70) | data formatting | bytes 12582912 | tf_op jit(solution)/shard_map/reshape;reshape | solution.py:91
  196.6 20.7 %fusion.2 = f32[128,6,64,64]{2,3,1,0:T(8,128)} fusion(bf16[128,6,64,64]{3,2,1,0:T(8,128)(2,1)} %copy.45, bf16[128,6,64,64]{3,2,0,1:T(8,128)(2,1)} %reshape_reshape.3), kind=kOutput, calls=%fused_computation.3 | convolution fusion | flops 402653184 | bytes 25165824 | tf_op jit(solution)/shard_map/pckj,pcjr->pckr/dot_general | solution.py:94
  217.3 24.6 %copy.46 = f32[128,6,64,64]{3,2,1,0:T(8,128)} copy(f32[128,6,64,64]{2,3,1,0:T(8,128)} %fusion.2) | data formatting | bytes 25165824 | tf_op jit(solution)/shard_map/pckj,pcjr->pckr/dot_general | solution.py:94
  242.0 20.8 %reshape.44 = f32[768,4096]{1,0:T(8,128)} reshape(f32[128,6,64,64]{3,2,1,0:T(8,128)} %copy.46) | data formatting | bytes 25165824 | tf_op jit(solution)/shard_map/reshape | solution.py:99
  262.7 7.7 %fusion.24 = f32[28,4096]{1,0:T(8,128)S(1)} fusion(f32[768,4096]{1,0:T(8,128)} %reshape.44, s32[768]{0:T(1024)S(1)} %eq.49), kind=kOutput, calls=%fused_computation.32 | convolution fusion | flops 1056986112 | bytes 13044736 | tf_op jit(solution)/shard_map/dot_general | solution.py:98
  272.4 1.4 fusion.6
  (36 shorter events, 4.0 us)
Async XLA Ops:
  0.0 1.0 copy-start
  10.9 20.4 %copy-start.1 = (bf16[16,256,64]{1,2,0:T(8,128)(2,1)S(1)}, bf16[16,256,64]{1,2,0:T(8,128)(2,1)}, u32[]{:S(2)}) copy-start(bf16[16,256,64]{1,2,0:T(8,128)(2,1)} %param.8) | copy-start | bytes 1572868
  21.1 148.1 %all-to-all-start = ((bf16[128,1,1,6,4096]{4,3,2,1,0:T(8,128)(2,1)}), bf16[128,1,1,6,4096]{4,3,2,1,0:T(8,128)(2,1)}, u32[]{:S(2)}, u32[]{:S(2)}) async-start(bf16[128,1,1,6,4096]{4,3,2,1,0:T(8,128)(2,1)} %bitcast.69), calls=%async_computation | async-start | bytes 16777216 | tf_op jit(solution)/shard_map/all_to_all | solution.py:26
  31.4 24.6 %copy-start.4 = (s32[1,128,6]{1,0,2:T(1,128)S(1)}, s32[1,128,6]{1,0,2:T(1,128)}, u32[]{:S(2)}) copy-start(s32[1,128,6]{1,0,2:T(1,128)} %param.15) | copy-start | bytes 9220
  31.4 24.9 %copy-start.3 = (s32[16,6]{0,1:T(8,128)S(1)}, s32[16,6]{0,1:T(8,128)}, u32[]{:S(2)}) copy-start(s32[16,6]{0,1:T(8,128)} %param.12) | copy-start | bytes 1156
  31.4 110.8 %collective-permute-start = (bf16[8,256,64]{1,2,0:T(8,128)(2,1)S(1)}, bf16[8,256,64]{1,2,0:T(8,128)(2,1)S(1)}, u32[]{:S(2)}, u32[]{:S(2)}) collective-permute-start(bf16[8,256,64]{1,2,0:T(8,128)(2,1)S(1)} %get-tuple-element.5), channel_id=1, source_target_pairs={{0,1},{1,2},{2,3},{3,4},{4,5},{5,6},{6,7},{7,8},{8,9},{9,10},{10,1... | collective-permute-start | bytes 786440 | tf_op jit(solution)/shard_map/ppermute | solution.py:39
  34.8 107.4 %collective-permute-start.1 = (bf16[8,256,64]{1,2,0:T(8,128)(2,1)S(1)}, bf16[8,256,64]{1,2,0:T(8,128)(2,1)S(1)}, u32[]{:S(2)}, u32[]{:S(2)}) collective-permute-start(bf16[8,256,64]{1,2,0:T(8,128)(2,1)S(1)} %get-tuple-element.6), channel_id=1, source_target_pairs={{1,0},{2,1},{3,2},{4,3},{5,4},{6,5},{7,6},{8,7},{9,8},{10,9},{11,1... | collective-permute-start | bytes 786440 | tf_op jit(solution)/shard_map/ppermute | solution.py:40
  262.7 8.7 %copy-start.2 = (bf16[1,24,64,64]{3,2,1,0:T(8,128)(2,1)S(1)}, bf16[1,24,64,64]{3,2,1,0:T(8,128)(2,1)}, u32[]{:S(2)}) copy-start(bf16[1,24,64,64]{3,2,1,0:T(8,128)(2,1)} %param.10) | copy-start | bytes 589828
where the time goes:
time: 276 us; the launch traced here: 274 us
  local copies, waits for them, and re-layouts  119 us (43%)
  waiting for transfers between devices  85.8 us (31%)
  matrix products  51.2 us (19%)
  starting transfers between devices  16.3 us (6%)
    ppermute x1, waiting for transfers between devices, with_halo(): lax.ppermute(last, axis, up)  85.8 us
    dot_general x1, local copies, waits for them, and re-layouts, shards(): jnp.einsum('pckj,pcjr->pckr', coupling[0], fetched, preferred_element_typ...  24.6 us
    reshape x1, local copies, waits for them, and re-layouts, shards(): products.reshape(peers * slots, rank * width)  20.8 us
    dot_general x1, matrix products, shards(): jnp.einsum('pckj,pcjr->pckr', coupling[0], fetched, preferred_element_typ...  20.7 us
    squeeze x1, local copies, waits for them, and re-layouts, shards(): coupling[0]  18.5 us
    another operation x1, local copies, waits for them, and re-layouts, shards(): exchange_both(shaped, ('gx', 'gy'), ('gx', 'gy'), (0, 1), (0, 1))  17.9 us
    all_to_all x1, starting transfers between devices, exchange_both(): tiles = lax.all_to_all(tiles, axis, split_axis=0, concat_axis=0, tiled=True)  10.2 us
    another operation x1, local copies, waits for them, and re-layouts, exchange_both(): tiles = tiles.reshape(-1, *inside)  10.2 us
  transfers between devices with their start and end apart: 3, of which 1 were waited for; matrix products, arithmetic and copies ran while one was open for 17% of the time, Pallas kernels for 0%

commit v1 on v0

v1 whole, which is shorter than its diff:
```python
import functools

import jax
import jax.numpy as jnp
from jax import lax
from jax.experimental import pallas as pl
from jax.experimental.pallas import tpu as pltpu
from jax.sharding import PartitionSpec as P

AXES = ("gx", "gy")
LEVELS = 3
F32 = jnp.float32
BF16 = jnp.bfloat16


def level_bounds(leaves):
    bounds, offset = [], 0
    for depth in range(LEVELS):
        bounds.append((offset, leaves >> depth))
        offset += leaves >> depth
    return bounds, offset


def contract(a, b, da, db):
    return lax.dot_general(a, b, (((da,), (db,)), ((), ())), preferred_element_type=F32)


def split_pair(x):
    high = x.astype(BF16)
    return high, (x - high.astype(F32)).astype(BF16)


def up_kernel(bounds, slots, per_step, send, charges, basis, transfer, out, upward):
    half = upward.shape[1]
    step = pl.program_id(0)

    @pl.when(step == 0)
    def _():
        def put(c, block):
            block = block.astype(BF16)
            upward[c] = jnp.concatenate([block[:half], block[half:]], axis=1)
            return block

        held = []
        for leaf in range(bounds[0][1]):
            held.append(put(leaf, contract(basis[leaf], charges[leaf], 1, 1)))
        for depth in range(LEVELS - 1):
            lo, size = bounds[depth]
            above = bounds[depth + 1][0]
            parents = []
            for c in range(size // 2):
                both = jnp.concatenate([transfer[lo + 2 * c], transfer[lo + 2 * c + 1]], axis=0)
                kids = jnp.concatenate([held[2 * c], held[2 * c + 1]], axis=0)
                parents.append(put(above + c, contract(both, kids, 0, 0)))
            held = parents

    def copy(i, carry):
        d = step * per_step + i
        for c in range(slots):
            out[pl.ds((i * slots + c) * half, half), :] = upward[send[c, d]]
        return carry

    lax.fori_loop(0, per_step, copy, 0, unroll=4)


def near_kernel(first, source, low, own, high, blocks, out, window):
    leaf = pl.program_id(0)
    reach, leaves = low.shape[0], own.shape[0]

    @pl.when(leaf == 0)
    def _():
        window[pl.ds(0, reach)] = low[...]
        window[pl.ds(reach, leaves)] = own[...]
        window[pl.ds(reach + leaves, reach)] = high[...]

    total = None
    for s in range(blocks.shape[1]):
        row = source[s, leaf] - first[0] + reach
        term = contract(window[row], blocks[0, s], 1, 1)
        total = term if total is None else total + term
    out[0] = total


def far_kernel(bounds, slots, peers, target, coupling, fetched, basis, transfer, near, out, acc):
    half = 32
    step = pl.program_id(0)

    @pl.when(step == 0)
    def _():
        acc[...] = jnp.zeros_like(acc)

    for i in range(peers):
        for c in range(slots):
            v = fetched[pl.ds((i * slots + c) * half, half), :]
            u = jnp.concatenate([v, pltpu.roll(v, 64, 1)], axis=0)
            product = contract(coupling[i, c], u, 1, 0)
            acc[target[c, step * peers + i]] += product

    @pl.when(step == pl.num_programs(0) - 1)
    def _():
        rank = basis.shape[1]
        down = [acc[c][:, :rank] for c in range(bounds[-1][0] + bounds[-1][1])]
        for depth in range(LEVELS - 2, -1, -1):
            lo, size = bounds[depth]
            above = bounds[depth + 1][0]
            for c in range(size):
                high, low = split_pair(down[above + c // 2])
                matrix = transfer[lo + c]
                down[lo + c] = down[lo + c] + contract(matrix, high, 1, 0) + contract(matrix, low, 1, 0)
        for leaf in range(bounds[0][1]):
            high, low = split_pair(down[leaf])
            far_leaf = contract(high, basis[leaf], 0, 0) + contract(low, basis[leaf], 0, 0)
            out[leaf] = (near[leaf] + far_leaf).astype(BF16)


def whole(shape):
    return pl.BlockSpec(shape, lambda *_: (0,) * len(shape))


def shards(
    charges, leaf_basis, transfer, near_blocks, near_source, coupling, send_cluster, target_cluster
):
    leaves, panels, width = charges.shape
    rank = leaf_basis.shape[2]
    peers, slots = send_cluster.shape[1:]
    near = near_source.shape[1]
    bounds, clusters = level_bounds(leaves)
    half = rank * width // 128
    reach = leaves // 2
    outer, inner = lax.axis_size("gx"), lax.axis_size("gy")
    count = outer * inner

    charges_t = jnp.swapaxes(charges, 1, 2)
    basis_t = jnp.swapaxes(leaf_basis, 1, 2)
    matrices = transfer[0]
    send = jnp.transpose(send_cluster[0], (1, 0))
    target = jnp.transpose(target_cluster[0], (1, 0))
    source = jnp.transpose(near_source, (1, 0))

    up = [(i, i + 1) for i in range(count - 1)]
    low = lax.ppermute(charges_t[leaves - reach :], AXES, up)
    high = lax.ppermute(charges_t[:reach], AXES, [(b, a) for a, b in up])

    steps = 8
    per_step = peers // steps
    packed = pl.pallas_call(
        functools.partial(up_kernel, bounds, slots, per_step),
        grid_spec=pltpu.PrefetchScalarGridSpec(
            num_scalar_prefetch=1,
            grid=(steps,),
            in_specs=[
                whole((leaves, width, panels)),
                whole((leaves, rank, panels)),
                whole(matrices.shape),
            ],
            out_specs=pl.BlockSpec((per_step * slots * half, 128), lambda i, *_: (i, 0)),
            scratch_shapes=[pltpu.VMEM((clusters, half, 128), BF16)],
        ),
        out_shape=jax.ShapeDtypeStruct((peers * slots * half, 128), BF16),
        name="up_pick",
    )(send, charges_t, basis_t, matrices)

    packed, low, high = lax.optimization_barrier((packed, low, high))
    fetched = lax.all_to_all(packed, AXES, split_axis=0, concat_axis=0, tiled=True)

    first = (lax.axis_index(AXES) * leaves).reshape(1)
    near_field = pl.pallas_call(
        near_kernel,
        grid_spec=pltpu.PrefetchScalarGridSpec(
            num_scalar_prefetch=2,
            grid=(leaves,),
            in_specs=[
                whole((reach, width, panels)),
                whole((leaves, width, panels)),
                whole((reach, width, panels)),
                pl.BlockSpec((1, near, panels, panels), lambda i, *_: (i, 0, 0, 0)),
            ],
            out_specs=pl.BlockSpec((1, width, panels), lambda i, *_: (i, 0, 0)),
            scratch_shapes=[pltpu.VMEM((leaves + 2 * reach, width, panels), BF16)],
        ),
        out_shape=jax.ShapeDtypeStruct((leaves, width, panels), F32),
        cost_estimate=pl.CostEstimate(
            flops=2 * leaves * near * panels * panels * width,
            bytes_accessed=2 * leaves * near * panels * panels,
            transcendentals=0,
        ),
        name="near",
    )(first, source, low, charges_t, high, near_blocks)

    fsteps = 16
    fpeers = peers // fsteps
    potential_t = pl.pallas_call(
        functools.partial(far_kernel, bounds, slots, fpeers),
        grid_spec=pltpu.PrefetchScalarGridSpec(
            num_scalar_prefetch=1,
            grid=(fsteps,),
            in_specs=[
                pl.BlockSpec((fpeers, slots, rank, rank), lambda i, *_: (i, 0, 0, 0)),
                pl.BlockSpec((fpeers * slots * half, 128), lambda i, *_: (i, 0)),
                whole((leaves, rank, panels)),
                whole(matrices.shape),
                whole((leaves, width, panels)),
            ],
            out_specs=whole((leaves, width, panels)),
            scratch_shapes=[pltpu.VMEM((clusters + 1, rank, 128), F32)],
        ),
        out_shape=jax.ShapeDtypeStruct((leaves, width, panels), BF16),
        name="far",
    )(target, coupling[0], fetched, basis_t, matrices, near_field)
    return jnp.swapaxes(potential_t, 1, 2)


def solution(mesh):
    placed = (
        P(AXES, None, None),
        P(AXES, None, None),
        P(AXES, None, None, None),
        P(AXES, None, None, None),
        P(AXES, None),
        P(AXES, None, None, None, None),
        P(AXES, None, None),
        P(AXES, None, None),
    )
    return jax.shard_map(
        shards, mesh=mesh, in_specs=placed, out_specs=P(AXES, None, None), check_vma=False
    )
```

time: 276 us -> 127 us (0.46)
  the two profiles are of different devices: /device:TPU:106 before, /device:TPU:10 now
where the time goes in v1:
time: 127 us; the launch traced here: 126 us
  waiting for transfers between devices  44.7 us (35%)
  Pallas kernels  41 us (32%)
  local copies, waits for them, and re-layouts  22.1 us (17%)
  starting transfers between devices  17.9 us (14%)
    all_to_all x1, waiting for transfers between devices, shards(): lax.all_to_all(packed, AXES, split_axis=0, concat_axis=0, tiled=True)  42.7 us
    unnamed x9, local copies, waits for them, and re-layouts  21 us
    pallas_call x1, Pallas kernels, shards(): pl.pallas_call(functools.partial(far_kernel, bounds, slots, fpeers), grid...  18.3 us
    pallas_call x1, Pallas kernels, shards(): pl.pallas_call(near_kernel, grid_spec=pltpu.PrefetchScalarGridSpec(num_sc...  14.9 us
    all_to_all x1, starting transfers between devices, shards(): lax.all_to_all(packed, AXES, split_axis=0, concat_axis=0, tiled=True)  12 us
    pallas_call x1, Pallas kernels, shards(): pl.pallas_call(functools.partial(up_kernel, bounds, slots, per_step), gri...  7.83 us
    ppermute x1, starting transfers between devices, shards(): low = lax.ppermute(charges_t[leaves - reach:], AXES, up)  3.4 us
  transfers between devices with their start and end apart: 3, of which 2 were waited for; matrix products, arithmetic and copies ran while one was open for 16% of the time, Pallas kernels for 18%

profile of v1, /device:TPU:10, one launch (start us, length us, event | category | flops | bytes accessed | tf_op | source)
XLA Modules:
  0.0 125.8 jit_solution(15261783351992771268)
XLA Ops:
  0.0 1.1 fusion
  1.1 2.4 %collective-permute-start.1 = (bf16[8,64,256]{2,1,0:T(8,128)(2,1)S(1)}, bf16[8,64,256]{2,1,0:T(8,128)(2,1)S(1)}, u32[]{:S(2)}, u32[]{:S(2)}) collective-permute-start(bf16[8,64,256]{2,1,0:T(8,128)(2,1)S(1)} %get-tuple-element.11), channel_id=1, source_target_pairs={{1,0},{2,1},{3,2},{4,3},{5,4},{6,5},{7,6},{8,7},{9,8},{10,9},{11,1... | collective-permute-start | bytes 786440 | tf_op jit(solution)/shard_map/ppermute | solution.py:142
  3.5 3.4 %collective-permute-start = (bf16[8,64,256]{2,1,0:T(8,128)(2,1)S(1)}, bf16[8,64,256]{2,1,0:T(8,128)(2,1)S(1)}, u32[]{:S(2)}, u32[]{:S(2)}) collective-permute-start(bf16[8,64,256]{2,1,0:T(8,128)(2,1)S(1)} %get-tuple-element.12), channel_id=1, source_target_pairs={{0,1},{1,2},{2,3},{3,4},{4,5},{5,6},{6,7},{7,8},{8,9},{9,10},{10,1... | collective-permute-start | bytes 786440 | tf_op jit(solution)/shard_map/ppermute | solution.py:141
  6.9 1.3 %copy.14 = s32[1,128,6]{1,2,0:T(8,128)} copy(s32[1,128,6]{1,0,2:T(1,128)} %param.14) | data formatting | bytes 6144
  8.2 7.8 %up_pick.1 = bf16[24576,128]{1,0:T(8,128)(2,1)} custom-call(s32[6,128]{1,0:T(8,128)} %bitcast.28, bf16[16,64,256]{2,1,0:T(8,128)(2,1)} %bitcast.22, bf16[16,64,256]{2,1,0:T(8,128)(2,1)} %bitcast.24, bf16[24,64,64]{2,1,0:T(8,128)(2,1)} %bitcast.26), custom_call_target="tpu_custom_call" | custom-call | tf_op jit(solution)/shard_map/up_pick/pallas_call | solution.py:146
  16.0 0.0 collective-permute-done.1.high
  16.0 0.0 copy-start
  16.0 2.0 %collective-permute-done.low = bf16[8,64,256]{2,1,0:T(8,128)(2,1)S(1)} collective-permute-done((bf16[8,64,256]{2,1,0:T(8,128)(2,1)S(1)}, bf16[8,64,256]{2,1,0:T(8,128)(2,1)S(1)}, u32[]{:S(2)}, u32[]{:S(2)}) %collective-permute-start) | collective-permute-done | bytes 262176 | tf_op jit(solution)/shard_map/ppermute | solution.py:141
  18.0 0.0 copy-start.1
  18.0 0.0 copy-start.2
  18.0 0.0 copy-done
  18.0 0.7 copy-done.1
  18.7 12.0 %all-to-all-start = ((bf16[128,192,128]{2,1,0:T(8,128)(2,1)}), bf16[128,192,128]{2,1,0:T(8,128)(2,1)}, u32[]{:S(2)}, u32[]{:S(2)}) async-start(bf16[128,192,128]{2,1,0:T(8,128)(2,1)} %bitcast.20), calls=%async_computation | async-start | bytes 12582912 | tf_op jit(solution)/shard_map/all_to_all | solution.py:164
  30.8 0.0 copy-done.2
  30.8 0.6 copy.15
  31.4 18.5 %copy.9 = bf16[1,128,6,64,64]{4,3,2,1,0:T(8,128)(2,1)} copy(bf16[1,128,6,64,64]{1,4,3,2,0:T(8,128)(2,1)} %param.13) | data formatting | bytes 12582912 | tf_op args[5]
  49.9 14.9 %near.1 = f32[16,64,256]{2,1,0:T(8,128)} custom-call(s32[1]{0:T(128)} %bitcast.8.first, s32[6,16]{1,0:T(8,128)} %bitcast.30, bf16[8,64,256]{2,1,0:T(8,128)(2,1)} %copy-done.1, bf16[16,64,256]{2,1,0:T(8,128)(2,1)} %bitcast.23, bf16[8,64,256]{2,1,0:T(8,128)(2,1)} %copy-done, bf16[16,6,256,256]{3,2,1,0:T(8,128)(2,1)} %blocks.1), custom_call_target="tpu_custom_call" | custom-call | flops 805306368 | bytes 12582912 | tf_op jit(solution)/shard_map/near/pallas_call | solution.py:167
  64.7 42.7 %all-to-all-done = bf16[128,192,128]{2,1,0:T(8,128)(2,1)} async-done(((bf16[128,192,128]{2,1,0:T(8,128)(2,1)}), bf16[128,192,128]{2,1,0:T(8,128)(2,1)}, u32[]{:S(2)}, u32[]{:S(2)}) %all-to-all-start) | async-done | bytes 6291488 | tf_op jit(solution)/shard_map/all_to_all | solution.py:164
  107.4 18.3 %far.1 = bf16[16,64,256]{2,1,0:T(8,128)(2,1)} custom-call(s32[6,128]{1,0:T(8,128)} %bitcast.29, bf16[128,6,64,64]{3,2,1,0:T(8,128)(2,1)} %bitcast.19, bf16[24576,128]{1,0:T(8,128)(2,1)} %bitcast.7.fetched, bf16[16,64,256]{2,1,0:T(8,128)(2,1)} %bitcast.25, bf16[24,64,64]{2,1,0:T(8,128)(2,1)} %bitcast.27, f32[16,64,256]{2,1,0:T(8,128)} %near.1), custom_call_target="tpu_custom_call" | custom-call | tf_op jit(solution)/shard_map/far/pallas_call | solution.py:192
Async XLA Ops:
  1.1 15.0 %collective-permute-start.1 = (bf16[8,64,256]{2,1,0:T(8,128)(2,1)S(1)}, bf16[8,64,256]{2,1,0:T(8,128)(2,1)S(1)}, u32[]{:S(2)}, u32[]{:S(2)}) collective-permute-start(bf16[8,64,256]{2,1,0:T(8,128)(2,1)S(1)} %get-tuple-element.11), channel_id=1, source_target_pairs={{1,0},{2,1},{3,2},{4,3},{5,4},{6,5},{7,6},{8,7},{9,8},{10,9},{11,1... | collective-permute-start | bytes 786440 | tf_op jit(solution)/shard_map/ppermute | solution.py:142
  3.5 14.5 %collective-permute-start = (bf16[8,64,256]{2,1,0:T(8,128)(2,1)S(1)}, bf16[8,64,256]{2,1,0:T(8,128)(2,1)S(1)}, u32[]{:S(2)}, u32[]{:S(2)}) collective-permute-start(bf16[8,64,256]{2,1,0:T(8,128)(2,1)S(1)} %get-tuple-element.12), channel_id=1, source_target_pairs={{0,1},{1,2},{2,3},{3,4},{4,5},{5,6},{6,7},{7,8},{8,9},{9,10},{10,1... | collective-permute-start | bytes 786440 | tf_op jit(solution)/shard_map/ppermute | solution.py:141
  16.0 2.0 %copy-start = (bf16[8,64,256]{2,1,0:T(8,128)(2,1)}, bf16[8,64,256]{2,1,0:T(8,128)(2,1)S(1)}, u32[]{:S(2)}) copy-start(bf16[8,64,256]{2,1,0:T(8,128)(2,1)S(1)} %collective-permute-done.1.high) | copy-start | bytes 786436
  18.0 0.7 copy-start.1
  18.0 12.8 %copy-start.2 = (s32[1,128,6]{1,0,2:T(1,128)S(1)}, s32[1,128,6]{1,0,2:T(1,128)}, u32[]{:S(2)}) copy-start(s32[1,128,6]{1,0,2:T(1,128)} %param.15) | copy-start | bytes 9220
  18.7 88.7 %all-to-all-start = ((bf16[128,192,128]{2,1,0:T(8,128)(2,1)}), bf16[128,192,128]{2,1,0:T(8,128)(2,1)}, u32[]{:S(2)}, u32[]{:S(2)}) async-start(bf16[128,192,128]{2,1,0:T(8,128)(2,1)} %bitcast.20), calls=%async_computation | async-start | bytes 12582912 | tf_op jit(solution)/shard_map/all_to_all | solution.py:164

commit v2 on v1

v2 whole, which is shorter than its diff:
```python
import functools

import jax
import jax.numpy as jnp
from jax import lax
from jax.experimental import pallas as pl
from jax.experimental.pallas import tpu as pltpu
from jax.sharding import PartitionSpec as P

AXES = ("gx", "gy")
LEVELS = 3
F32 = jnp.float32
BF16 = jnp.bfloat16


def level_bounds(leaves):
    bounds, offset = [], 0
    for depth in range(LEVELS):
        bounds.append((offset, leaves >> depth))
        offset += leaves >> depth
    return bounds, offset


def contract(a, b, da, db):
    return lax.dot_general(a, b, (((da,), (db,)), ((), ())), preferred_element_type=F32)


def split_pair(x):
    high = x.astype(BF16)
    return high, (x - high.astype(F32)).astype(BF16)


def up_kernel(bounds, slots, send, charges, basis, transfer, out, upward, staged, sems):
    half = upward.shape[1]
    chunks, rows = staged.shape[:2]
    per_chunk = rows // (slots * half)

    def put(c, block):
        block = block.astype(BF16)
        upward[c] = jnp.concatenate([block[:half], block[half:]], axis=1)
        return block

    held = []
    for leaf in range(bounds[0][1]):
        held.append(put(leaf, contract(basis[leaf], charges[leaf], 1, 1)))
    for depth in range(LEVELS - 1):
        lo, size = bounds[depth]
        above = bounds[depth + 1][0]
        parents = []
        for c in range(size // 2):
            both = jnp.concatenate([transfer[lo + 2 * c], transfer[lo + 2 * c + 1]], axis=0)
            kids = jnp.concatenate([held[2 * c], held[2 * c + 1]], axis=0)
            parents.append(put(above + c, contract(both, kids, 0, 0)))
        held = parents

    def send_out(j):
        rows_out = out.at[pl.ds(pl.multiple_of(j * rows, rows), rows)]
        return pltpu.make_async_copy(staged.at[j], rows_out, sems.at[j])

    @pl.loop(0, chunks)
    def _(j):
        def copy(i, carry):
            for c in range(slots):
                at = pl.multiple_of((i * slots + c) * half, half)
                staged[j, pl.ds(at, half), :] = upward[send[c, 0, j * per_chunk + i]]
            return carry

        lax.fori_loop(0, per_chunk, copy, 0, unroll=4)
        send_out(j).start()

    @pl.loop(0, chunks)
    def _(j):
        send_out(j).wait()


def near_kernel(first, source, low, own, high, blocks, out, window):
    step = pl.program_id(0)
    reach, leaves = low.shape[0], own.shape[0]
    per_step, near = blocks.shape[:2]

    @pl.when(step == 0)
    def _():
        window[pl.ds(0, reach)] = low[...]
        window[pl.ds(reach, leaves)] = own[...]
        window[pl.ds(reach + leaves, reach)] = high[...]

    for i in range(per_step):
        total = None
        for s in range(near):
            row = source[s, step * per_step + i] - first[0] + reach
            term = contract(window[row], blocks[i, s], 1, 1)
            total = term if total is None else total + term
        out[i] = total


def far_kernel(
    bounds, slots, chunks, target, coupling, fetched, basis, transfer, near, out,
    cbuf, fbuf, bbuf, tbuf, nbuf, acc, csem, fsem, esem,
):
    peers = cbuf.shape[0] // chunks
    half = fbuf.shape[0] // (cbuf.shape[0] * slots)
    rows = peers * slots * half

    def fetch(j):
        some = pl.ds(pl.multiple_of(j * peers, peers), peers)
        some_rows = pl.ds(pl.multiple_of(j * rows, rows), rows)
        return (
            pltpu.make_async_copy(coupling.at[some], cbuf.at[some], csem.at[j]),
            pltpu.make_async_copy(fetched.at[some_rows], fbuf.at[some_rows], fsem.at[j]),
        )

    extra = [
        pltpu.make_async_copy(source, held, esem.at[i])
        for i, (source, held) in enumerate(((transfer, tbuf), (basis, bbuf), (near, nbuf)))
    ]

    @pl.loop(0, chunks)
    def _(j):
        for copy in fetch(j):
            copy.start()

    for copy in extra:
        copy.start()
    acc[...] = jnp.zeros_like(acc)

    @pl.loop(0, chunks)
    def _(j):
        for copy in fetch(j):
            copy.wait()
        for i in range(peers):
            p = j * peers + i
            for c in range(slots):
                at = pl.multiple_of((p * slots + c) * half, half)
                v = fbuf[pl.ds(at, half), :]
                u = jnp.concatenate([v, pltpu.roll(v, 64, 1)], axis=0)
                acc[target[c, 0, p]] += contract(cbuf[p, c], u, 1, 0)

    for copy in extra:
        copy.wait()
    rank = bbuf.shape[1]
    down = [acc[c][:, :rank] for c in range(bounds[-1][0] + bounds[-1][1])]
    for depth in range(LEVELS - 2, -1, -1):
        lo, size = bounds[depth]
        above = bounds[depth + 1][0]
        for c in range(size):
            high, low = split_pair(down[above + c // 2])
            matrix = tbuf[lo + c]
            down[lo + c] = down[lo + c] + contract(matrix, high, 1, 0) + contract(matrix, low, 1, 0)
    for leaf in range(bounds[0][1]):
        high, low = split_pair(down[leaf])
        far_leaf = contract(high, bbuf[leaf], 0, 0) + contract(low, bbuf[leaf], 0, 0)
        out[leaf] = (nbuf[leaf] + far_leaf).astype(BF16)


def whole(shape):
    return pl.BlockSpec(shape, lambda *_: (0,) * len(shape))


def shards(
    charges, leaf_basis, transfer, near_blocks, near_source, coupling, send_cluster, target_cluster
):
    leaves, panels, width = charges.shape
    rank = leaf_basis.shape[2]
    peers, slots = send_cluster.shape[1:]
    near = near_source.shape[1]
    bounds, clusters = level_bounds(leaves)
    half = rank * width // 128
    reach = leaves // 2
    outer, inner = lax.axis_size("gx"), lax.axis_size("gy")
    count = outer * inner

    charges_t = jnp.swapaxes(charges, 1, 2)
    basis_t = jnp.swapaxes(leaf_basis, 1, 2)
    matrices = transfer[0]
    send = jnp.transpose(send_cluster, (2, 0, 1))
    target = jnp.transpose(target_cluster, (2, 0, 1))
    source = jnp.transpose(near_source, (1, 0))

    up = [(i, i + 1) for i in range(count - 1)]
    low = lax.ppermute(charges_t[leaves - reach :], AXES, up)
    high = lax.ppermute(charges_t[:reach], AXES, [(b, a) for a, b in up])

    chunks = 8
    packed = pl.pallas_call(
        functools.partial(up_kernel, bounds, slots),
        grid_spec=pltpu.PrefetchScalarGridSpec(
            num_scalar_prefetch=1,
            grid=(),
            in_specs=[pl.BlockSpec(memory_space=pltpu.VMEM)] * 3,
            out_specs=pl.BlockSpec(memory_space=pl.ANY),
            scratch_shapes=[
                pltpu.VMEM((clusters, half, 128), BF16),
                pltpu.VMEM((chunks, peers * slots * half // chunks, 128), BF16),
                pltpu.SemaphoreType.DMA((chunks,)),
            ],
        ),
        out_shape=jax.ShapeDtypeStruct((peers * slots * half, 128), BF16),
        cost_estimate=pl.CostEstimate(
            flops=2 * leaves * panels * rank * width,
            bytes_accessed=2 * peers * slots * rank * width,
            transcendentals=0,
        ),
        name="up_pick",
    )(send, charges_t, basis_t, matrices)

    packed, low, high = lax.optimization_barrier((packed, low, high))
    fetched = lax.all_to_all(packed, AXES, split_axis=0, concat_axis=0, tiled=True)

    per_step = 4
    first = (lax.axis_index(AXES) * leaves).reshape(1)
    near_field = pl.pallas_call(
        near_kernel,
        grid_spec=pltpu.PrefetchScalarGridSpec(
            num_scalar_prefetch=2,
            grid=(leaves // per_step,),
            in_specs=[
                whole((reach, width, panels)),
                whole((leaves, width, panels)),
                whole((reach, width, panels)),
                pl.BlockSpec((per_step, near, panels, panels), lambda i, *_: (i, 0, 0, 0)),
            ],
            out_specs=pl.BlockSpec((per_step, width, panels), lambda i, *_: (i, 0, 0)),
            scratch_shapes=[pltpu.VMEM((leaves + 2 * reach, width, panels), BF16)],
        ),
        out_shape=jax.ShapeDtypeStruct((leaves, width, panels), F32),
        cost_estimate=pl.CostEstimate(
            flops=2 * leaves * near * panels * panels * width,
            bytes_accessed=2 * leaves * near * panels * panels,
            transcendentals=0,
        ),
        name="near",
    )(first, source, low, charges_t, high, near_blocks)

    fchunks = 16
    potential_t = pl.pallas_call(
        functools.partial(far_kernel, bounds, slots, fchunks),
        grid_spec=pltpu.PrefetchScalarGridSpec(
            num_scalar_prefetch=1,
            grid=(),
            in_specs=[pl.BlockSpec(memory_space=pl.ANY)] * 5,
            out_specs=pl.BlockSpec(memory_space=pltpu.VMEM),
            scratch_shapes=[
                pltpu.VMEM((peers, slots, rank, rank), BF16),
                pltpu.VMEM((peers * slots * half, 128), BF16),
                pltpu.VMEM((leaves, rank, panels), BF16),
                pltpu.VMEM(matrices.shape, BF16),
                pltpu.VMEM((leaves, width, panels), F32),
                pltpu.VMEM((clusters + 1, rank, 128), F32),
                pltpu.SemaphoreType.DMA((fchunks,)),
                pltpu.SemaphoreType.DMA((fchunks,)),
                pltpu.SemaphoreType.DMA((3,)),
            ],
        ),
        out_shape=jax.ShapeDtypeStruct((leaves, width, panels), BF16),
        name="far",
    )(target, coupling[0], fetched, basis_t, matrices, near_field)
    return jnp.swapaxes(potential_t, 1, 2)


def solution(mesh):
    placed = (
        P(AXES, None, None),
        P(AXES, None, None),
        P(AXES, None, None, None),
        P(AXES, None, None, None),
        P(AXES, None),
        P(AXES, None, None, None, None),
        P(AXES, None, None),
        P(AXES, None, None),
    )
    return jax.shard_map(
        shards, mesh=mesh, in_specs=placed, out_specs=P(AXES, None, None), check_vma=False
    )
```

time: 127 us -> 118 us (0.929)
  Pallas kernels: 41 us -> 27.7 us
  waiting for transfers between devices: 44.7 us -> 53.6 us
  local copies, waits for them, and re-layouts: 22.1 us -> 20.2 us
  starting transfers between devices: 17.9 us -> 16 us
    pallas_call x2, Pallas kernels: 26.2 us -> 18.6 us  [the longest x1 12.1 us: shards(): pl.pallas_call(functools.partial(far_kernel, bounds, slots, fchunks), gri...]
    all_to_all x1, waiting for transfers between devices: 42.7 us -> 49.1 us  [shards(): lax.all_to_all(packed, AXES, split_axis=0, concat_axis=0, tiled=True)]
    pallas_call x1, Pallas kernels: 14.9 us -> 9.08 us  [shards(): pl.pallas_call(near_kernel, grid_spec=pltpu.PrefetchScalarGridSpec(num_sc...]
    ppermute x1, waiting for transfers between devices: 1.99 us -> 4.53 us  [shards(): low = lax.ppermute(charges_t[leaves - reach:], AXES, up)]
    unnamed x9 -> x5, local copies, waits for them, and re-layouts: 21 us -> 19.2 us
    all_to_all x1, starting transfers between devices: 12 us -> 10.2 us  [shards(): lax.all_to_all(packed, AXES, split_axis=0, concat_axis=0, tiled=True)]
  transfers between devices with their start and end apart: 3 -> 3, of which waited for: 2 -> 2; matrix products, arithmetic and copies ran while one was open for 16% -> 16% of each run, Pallas kernels for 18% -> 13%
where the time goes in v2:
time: 118 us
  waiting for transfers between devices  53.6 us (45%)
  Pallas kernels  27.7 us (23%)
  local copies, waits for them, and re-layouts  20.2 us (17%)
  starting transfers between devices  16 us (14%)
    all_to_all x1, waiting for transfers between devices, shards(): lax.all_to_all(packed, AXES, split_axis=0, concat_axis=0, tiled=True)  49.1 us
    unnamed x5, local copies, waits for them, and re-layouts  19.2 us
    pallas_call x1, Pallas kernels, shards(): pl.pallas_call(functools.partial(far_kernel, bounds, slots, fchunks), gri...  12.1 us
    all_to_all x1, starting transfers between devices, shards(): lax.all_to_all(packed, AXES, split_axis=0, concat_axis=0, tiled=True)  10.2 us
    pallas_call x1, Pallas kernels, shards(): pl.pallas_call(near_kernel, grid_spec=pltpu.PrefetchScalarGridSpec(num_sc...  9.08 us
    pallas_call x1, Pallas kernels, shards(): pl.pallas_call(functools.partial(up_kernel, bounds, slots), grid_spec=plt...  6.55 us
    ppermute x1, waiting for transfers between devices, shards(): low = lax.ppermute(charges_t[leaves - reach:], AXES, up)  4.53 us
    ppermute x1, starting transfers between devices, shards(): low = lax.ppermute(charges_t[leaves - reach:], AXES, up)  3.4 us
  transfers between devices with their start and end apart: 3, of which 2 were waited for; matrix products, arithmetic and copies ran while one was open for 16% of the time, Pallas kernels for 13%

profile of v2, /device:TPU:10, one launch (start us, length us, event | category | flops | bytes accessed | tf_op | source)
XLA Modules:
  0.0 117.6 jit_solution(7088256606231224930)
XLA Ops:
  0.0 1.1 fusion
  1.1 2.4 %collective-permute-start.1 = (bf16[8,64,256]{2,1,0:T(8,128)(2,1)S(1)}, bf16[8,64,256]{2,1,0:T(8,128)(2,1)S(1)}, u32[]{:S(2)}, u32[]{:S(2)}) collective-permute-start(bf16[8,64,256]{2,1,0:T(8,128)(2,1)S(1)} %get-tuple-element.11), channel_id=1, source_target_pairs={{1,0},{2,1},{3,2},{4,3},{5,4},{6,5},{7,6},{8,7},{9,8},{10,9},{11,1... | collective-permute-start | bytes 786440 | tf_op jit(solution)/shard_map/ppermute | solution.py:181
  3.5 3.4 %collective-permute-start = (bf16[8,64,256]{2,1,0:T(8,128)(2,1)S(1)}, bf16[8,64,256]{2,1,0:T(8,128)(2,1)S(1)}, u32[]{:S(2)}, u32[]{:S(2)}) collective-permute-start(bf16[8,64,256]{2,1,0:T(8,128)(2,1)S(1)} %get-tuple-element.12), channel_id=1, source_target_pairs={{0,1},{1,2},{2,3},{3,4},{4,5},{5,6},{6,7},{7,8},{8,9},{9,10},{10,1... | collective-permute-start | bytes 786440 | tf_op jit(solution)/shard_map/ppermute | solution.py:180
  6.9 6.5 %up_pick.1 = bf16[24576,128]{1,0:T(8,128)(2,1)} custom-call(s32[6,1,128]{2,1,0:T(1,128)} %bitcast.21, bf16[16,64,256]{2,1,0:T(8,128)(2,1)} %bitcast.14, bf16[16,64,256]{2,1,0:T(8,128)(2,1)} %bitcast.16, bf16[24,64,64]{2,1,0:T(8,128)(2,1)} %bitcast.18), custom_call_target="tpu_custom_call" | custom-call | flops 33554432 | bytes 6291456 | tf_op jit(solution)/shard_map/up_pick/pallas_call | solution.py:184
  13.5 0.0 collective-permute-done.1.high
  13.5 0.0 copy-start
  13.5 4.5 %collective-permute-done.low = bf16[8,64,256]{2,1,0:T(8,128)(2,1)S(1)} collective-permute-done((bf16[8,64,256]{2,1,0:T(8,128)(2,1)S(1)}, bf16[8,64,256]{2,1,0:T(8,128)(2,1)S(1)}, u32[]{:S(2)}, u32[]{:S(2)}) %collective-permute-start) | collective-permute-done | bytes 262176 | tf_op jit(solution)/shard_map/ppermute | solution.py:180
  18.0 0.0 copy-start.1
  18.0 0.0 copy-done
  18.0 0.7 copy-done.1
  18.7 10.2 %all-to-all-start = ((bf16[128,192,128]{2,1,0:T(8,128)(2,1)}), bf16[128,192,128]{2,1,0:T(8,128)(2,1)}, u32[]{:S(2)}, u32[]{:S(2)}) async-start(bf16[128,192,128]{2,1,0:T(8,128)(2,1)} %bitcast.12), calls=%async_computation | async-start | bytes 12582912 | tf_op jit(solution)/shard_map/all_to_all | solution.py:207
  28.9 18.5 %copy.9 = bf16[1,128,6,64,64]{4,3,2,1,0:T(8,128)(2,1)} copy(bf16[1,128,6,64,64]{1,4,3,2,0:T(8,128)(2,1)} %param.13) | data formatting | bytes 12582912 | tf_op args[5]
  47.4 9.1 %near.1 = f32[16,64,256]{2,1,0:T(8,128)} custom-call(s32[1]{0:T(128)} %bitcast.8.first, s32[6,16]{1,0:T(8,128)} %bitcast.20, bf16[8,64,256]{2,1,0:T(8,128)(2,1)} %copy-done.1, bf16[16,64,256]{2,1,0:T(8,128)(2,1)} %bitcast.15, bf16[8,64,256]{2,1,0:T(8,128)(2,1)} %copy-done, bf16[16,6,256,256]{3,2,1,0:T(8,128)(2,1)} %blocks.1), custom_call_target="tpu_custom_call" | custom-call | flops 805306368 | bytes 12582912 | tf_op jit(solution)/shard_map/near/pallas_call | solution.py:211
  56.5 49.1 %all-to-all-done = bf16[128,192,128]{2,1,0:T(8,128)(2,1)} async-done(((bf16[128,192,128]{2,1,0:T(8,128)(2,1)}), bf16[128,192,128]{2,1,0:T(8,128)(2,1)}, u32[]{:S(2)}, u32[]{:S(2)}) %all-to-all-start) | async-done | bytes 6291488 | tf_op jit(solution)/shard_map/all_to_all | solution.py:207
  105.6 12.1 %far.1 = bf16[16,64,256]{2,1,0:T(8,128)(2,1)} custom-call(s32[6,1,128]{2,1,0:T(1,128)} %bitcast.22, bf16[128,6,64,64]{3,2,1,0:T(8,128)(2,1)} %bitcast.11, bf16[24576,128]{1,0:T(8,128)(2,1)} %bitcast.7.fetched, bf16[16,64,256]{2,1,0:T(8,128)(2,1)} %bitcast.17, bf16[24,64,64]{2,1,0:T(8,128)(2,1)} %bitcast.19, f32[16,64,256]{2,1,0:T(8,128)} %near.1), custom_call_target="tpu_custom_call" | custom-call | tf_op jit(solution)/shard_map/far/pallas_call | solution.py:235
Async XLA Ops:
  1.1 12.4 %collective-permute-start.1 = (bf16[8,64,256]{2,1,0:T(8,128)(2,1)S(1)}, bf16[8,64,256]{2,1,0:T(8,128)(2,1)S(1)}, u32[]{:S(2)}, u32[]{:S(2)}) collective-permute-start(bf16[8,64,256]{2,1,0:T(8,128)(2,1)S(1)} %get-tuple-element.11), channel_id=1, source_target_pairs={{1,0},{2,1},{3,2},{4,3},{5,4},{6,5},{7,6},{8,7},{9,8},{10,9},{11,1... | collective-permute-start | bytes 786440 | tf_op jit(solution)/shard_map/ppermute | solution.py:181
  3.5 14.5 %collective-permute-start = (bf16[8,64,256]{2,1,0:T(8,128)(2,1)S(1)}, bf16[8,64,256]{2,1,0:T(8,128)(2,1)S(1)}, u32[]{:S(2)}, u32[]{:S(2)}) collective-permute-start(bf16[8,64,256]{2,1,0:T(8,128)(2,1)S(1)} %get-tuple-element.12), channel_id=1, source_target_pairs={{0,1},{1,2},{2,3},{3,4},{4,5},{5,6},{6,7},{7,8},{8,9},{9,10},{10,1... | collective-permute-start | bytes 786440 | tf_op jit(solution)/shard_map/ppermute | solution.py:180
  13.5 4.5 %copy-start = (bf16[8,64,256]{2,1,0:T(8,128)(2,1)}, bf16[8,64,256]{2,1,0:T(8,128)(2,1)S(1)}, u32[]{:S(2)}) copy-start(bf16[8,64,256]{2,1,0:T(8,128)(2,1)S(1)} %collective-permute-done.1.high) | copy-start | bytes 786436
  18.0 0.7 copy-start.1
  18.7 86.8 %all-to-all-start = ((bf16[128,192,128]{2,1,0:T(8,128)(2,1)}), bf16[128,192,128]{2,1,0:T(8,128)(2,1)}, u32[]{:S(2)}, u32[]{:S(2)}) async-start(bf16[128,192,128]{2,1,0:T(8,128)(2,1)} %bitcast.12), calls=%async_computation | async-start | bytes 12582912 | tf_op jit(solution)/shard_map/all_to_all | solution.py:207
